TPU v7x, 256 devices: a whole 4x4x8 slice. The times are simulated.
256 devices in a mesh: node: 32 (over z, x), feat: 8 (over y, core).
Axes of the slice: x: 4, y: 4, z: 8, core: 2. Of those that a mesh axis runs over, the one named last changes fastest.
Arguments:
- out_grad: bfloat16 [256, 262144], P('feat', 'node'), may hold values from -6 to 6
- pre_act: bfloat16 [256, 262144], P('feat', 'node'), may hold values from -6 to 6
- in_act: bfloat16 [256, 262144], P(None, ('node', 'feat')), may hold values from -6 to 6
- weight: bfloat16 [256, 256], replicated, may hold values from -0.375 to 0.375
- tiles: bfloat16 [2048, 24, 128, 128], P('node'), may hold values from -0.4375 to 0.4375
- indices: int32 [2048, 24], P('node'), may hold values from 0 to 2047, as said below
- counts: int32 [2048], P('node'), may hold values from 1 to 24, as said below
Outputs:
- in_grad: bfloat16 [256, 262144], P(None, ('node', 'feat'))
- weight_grad: float32 [256, 256], replicated
Inputs may be any that keep to these rules, and one draw needn't show every extreme that they name: `indices`: the 24 column blocks named by one row block are distinct; slots at or after the row block's count are ignored. Each node device has a cap between 2 and 24, and its row blocks' counts are at most that cap, except for one row block in the whole graph whose count is 24.
All inputs are finite; a program needn't handle non-finite values.
Results may differ from a plain program's by a relative error of at most 0.012.
Values may be sent and summed in bfloat16 or wider, within the bound.
No kernel may reach another device: no remote copies, remote signals or barrier semaphores. Data moves between devices by JAX's collectives and lax.ppermute only.
A program may use at most 192 MiB of HBM per device.

v0:
```python
import jax
import jax.numpy as jnp
from jax import lax
from jax.sharding import PartitionSpec as P


def sent_to_all(shard, axis):
    size = lax.axis_size(axis)
    return lax.all_to_all(
        jnp.broadcast_to(shard[None], (size, *shard.shape)), axis, 0, 0, tiled=True
    )


def over_copies(shard, axis):
    everything = sent_to_all(shard, axis)
    return jnp.sum(everything.astype(jnp.float32), axis=0)


def laid_out(tiles, dim):
    lengths = list(tiles.shape[1:])
    lengths[dim] *= tiles.shape[0]
    return jnp.moveaxis(tiles, 0, dim).reshape(lengths)


def collect(shard, axis, dim):
    return laid_out(sent_to_all(shard, axis), dim)


def per_device(out_grad, pre_act, in_act, weight, tiles, indices, counts):
    grad_pre = jnp.where(pre_act > 0, out_grad, jnp.zeros_like(out_grad))
    whole = lax.all_gather(grad_pre, "node", axis=1, tiled=True)
    feat_rows = whole.shape[0]
    block_size = tiles.shape[2]
    slot_count = tiles.shape[1]
    local_rows = grad_pre.shape[1]
    blocks = whole.reshape(feat_rows, whole.shape[1] // block_size, block_size)
    picked = jnp.take(blocks, indices, axis=1)
    slots = jnp.arange(slot_count, dtype=jnp.int32)
    live = (slots[None, :] < counts[:, None]).astype(jnp.bfloat16)
    picked = picked * live[None, :, :, None]
    summed = jnp.einsum("frkc,rkic->fri", picked, tiles, preferred_element_type=jnp.float32)
    aggregated = summed.reshape(feat_rows, local_rows).astype(jnp.bfloat16)
    scale = float(whole.shape[1]) ** (-0.5)
    node_rows = lax.all_to_all(aggregated, "feat", split_axis=1, concat_axis=0, tiled=True)
    in_grad = jnp.dot(weight, node_rows, preferred_element_type=jnp.float32).astype(jnp.bfloat16)
    group_acts = lax.all_gather(in_act, "feat", axis=1, tiled=True)
    column_part = (
        lax.dot_general(
            group_acts, aggregated, (((1,), (1,)), ((), ())), preferred_element_type=jnp.float32
        )
        * scale
    )
    column_part = over_copies(column_part.astype(jnp.bfloat16), "node").astype(jnp.float32)
    weight_grad = collect(column_part.astype(jnp.bfloat16), "feat", 1).astype(column_part.dtype)
    return (in_grad, weight_grad)


def solution(mesh):
    in_specs = (
        P("feat", "node"),
        P("feat", "node"),
        P(None, ("node", "feat")),
        P(),
        P("node", None, None, None),
        P("node", None),
        P("node"),
    )
    out_specs = (P(None, ("node", "feat")), P())
    return jax.shard_map(
        per_device, mesh=mesh, in_specs=in_specs, out_specs=out_specs, check_vma=False
    )
```

profile of v0, /device:TPU:1, one launch (start us, length us, event | category | flops | bytes accessed | tf_op | source)
XLA Modules:
  0.0 266.6 jit_solution(17880768833656026010)
XLA Ops:
  7.2 2.1 compare_select_fusion
  9.4 0.7 all-gather.5.cloned.1.call-update
  10.1 0.7 compare_select_fusion.1
  11.0 0.7 compare_and_fusion
  11.8 0.7 fusion.18
  12.5 141.4 %all-gather.3.cloned.1.call-done = bf16[32,262144]{1,0:T(8,128)(2,1)} async-done(((bf16[32,8192]{1,0:T(8,128)(2,1)}), bf16[32,262144]{1,0:T(8,128)(2,1)}) %all-gather.3.cloned.1.call-update) | async-done | bytes 16777232 | tf_op jit(solution)/shard_map/all_gather | solution.py:31
  154.0 14.6 %copy_bitcast_fusion = bf16[32,2048,128]{2,0,1:T(8,128)(2,1)} fusion(bf16[32,262144]{1,0:T(8,128)(2,1)} %all-gather.3.cloned.1.call-done), kind=kLoop, calls=%fused_computation.1 | loop fusion | bytes 33554432 | tf_op jit(solution)/shard_map/reshape | solution.py:36
  168.6 12.9 %gather_fusion = bf16[1536,32,128]{2,1,0:T(8,128)(2,1)} fusion(bf16[32,2048,128]{2,0,1:T(8,128)(2,1)} %copy_bitcast_fusion, s32[2048]{0:T(1024)S(1)} %pad_clamp_fusion), kind=kCustom, calls=%fused_computation | custom fusion | bytes 25171968 | tf_op jit(solution)/shard_map/jit(_take)/gather | solution.py:37
  181.5 24.5 %fusion.10 = bf16[64,32,128]{2,1,0:T(8,128)(2,1)S(1)} fusion(bf16[64,24,128,128]{3,2,1,0:T(8,128)(2,1)} %param.11, bf16[64,24,32,128]{3,2,1,0:T(8,128)(2,1)} %bitcast.40, pred[64,24]{1,0:T(8,128)(4,1)S(1)} %copy.30, bf16[64,24]{1,0:T(8,128)(2,1)S(1)} %fusion.18), kind=kOutput, calls=%fused_computation.11 | convolution fusion | flops 1623457792 | bytes 63443456 | tf_op jit(solution)/shard_map/frkc,rkic->fri/dot_general | solution.py:41
  206.1 3.5 %fusion.15 = bf16[256,32]{0,1:T(8,128)(2,1)S(1)} fusion(bf16[256,8192]{1,0:T(8,128)(2,1)} %all-gather.5.cloned.1.call-done, bf16[64,32,128]{2,1,0:T(8,128)(2,1)S(1)} %fusion.10), kind=kOutput, calls=%fused_computation.15 | convolution fusion | flops 134234112 | bytes 4734976 | tf_op jit(solution)/shard_map/dot_general | solution.py:48
  209.6 0.9 broadcast_in_dim.30
  210.5 5.9 %all-to-all-start.1 = ((bf16[32,256,32]{1,2,0:T(8,128)(2,1)}), bf16[32,256,32]{1,2,0:T(8,128)(2,1)S(1)}, u32[]{:S(2)}, u32[]{:S(2)}) async-start(bf16[32,256,32]{1,2,0:T(8,128)(2,1)} %broadcast_in_dim.30), calls=%async_computation.1 | async-start | bytes 1048576 | tf_op jit(solution)/shard_map/all_to_all | solution.py:9
  216.3 0.2 copy.33
  216.6 0.2 convert_element_type.47
  216.8 1.1 copy.34
  217.9 13.9 %all-to-all-done.1 = bf16[32,256,32]{1,2,0:T(8,128)(2,1)S(1)} async-done(((bf16[32,256,32]{1,2,0:T(8,128)(2,1)}), bf16[32,256,32]{1,2,0:T(8,128)(2,1)S(1)}, u32[]{:S(2)}, u32[]{:S(2)}) %all-to-all-start.1) | async-done | bytes 524320 | tf_op jit(solution)/shard_map/all_to_all | solution.py:9
  231.8 7.6 %all-to-all-start = ((bf16[32,8,1024]{2,0,1:T(8,128)(2,1)}), bf16[32,8,1024]{2,0,1:T(8,128)(2,1)S(1)}, u32[]{:S(2)}, u32[]{:S(2)}) async-start(bf16[32,8,1024]{2,0,1:T(8,128)(2,1)} %copy.34), calls=%async_computation | async-start | bytes 1048576 | tf_op jit(solution)/shard_map/all_to_all | solution.py:44
  239.5 9.3 %all-to-all-done = bf16[32,8,1024]{2,0,1:T(8,128)(2,1)S(1)} async-done(((bf16[32,8,1024]{2,0,1:T(8,128)(2,1)}), bf16[32,8,1024]{2,0,1:T(8,128)(2,1)S(1)}, u32[]{:S(2)}, u32[]{:S(2)}) %all-to-all-start) | async-done | bytes 524320 | tf_op jit(solution)/shard_map/all_to_all | solution.py:44
  248.7 0.7 broadcast_in_dim.31
  249.4 4.2 %all-to-all-start.2 = ((bf16[8,256,32]{1,2,0:T(8,128)(2,1)}), bf16[8,256,32]{1,2,0:T(8,128)(2,1)S(1)}, u32[]{:S(2)}, u32[]{:S(2)}) async-start(bf16[8,256,32]{1,2,0:T(8,128)(2,1)} %broadcast_in_dim.31), calls=%async_computation.2 | async-start | bytes 262144 | tf_op jit(solution)/shard_map/all_to_all | solution.py:9
  253.6 0.3 fusion.13
  254.0 1.0 copy.36
  255.0 3.9 %all-to-all-done.2 = bf16[8,256,32]{1,2,0:T(8,128)(2,1)S(1)} async-done(((bf16[8,256,32]{1,2,0:T(8,128)(2,1)}), bf16[8,256,32]{1,2,0:T(8,128)(2,1)S(1)}, u32[]{:S(2)}, u32[]{:S(2)}) %all-to-all-start.2) | async-done | bytes 131104 | tf_op jit(solution)/shard_map/all_to_all | solution.py:9
  258.9 0.8 copy.37
  (12 shorter events, 0.5 us)
Async XLA Ops:
  7.2 246.5 %copy-start = (bf16[256,256]{1,0:T(8,128)(2,1)S(1)}, bf16[256,256]{1,0:T(8,128)(2,1)}, u32[]{:S(2)}) copy-start(bf16[256,256]{1,0:T(8,128)(2,1)} %param.10) | copy-start | bytes 393220
  7.2 146.8 %all-gather.3.cloned.1.call-start = ((), (), s32[]{:S(2)}) async-start(), calls=%async_computation.3 | async-start | bytes 17301504 | tf_op jit(solution)/shard_map/all_gather | solution.py:31
  9.3 196.7 %all-gather.5.cloned.1.call-start = ((), (), s32[]{:S(2)}) async-start(), calls=%async_computation.4 | async-start | bytes 4718592 | tf_op jit(solution)/shard_map/all_gather | solution.py:46
  210.5 21.3 %all-to-all-start.1 = ((bf16[32,256,32]{1,2,0:T(8,128)(2,1)}), bf16[32,256,32]{1,2,0:T(8,128)(2,1)S(1)}, u32[]{:S(2)}, u32[]{:S(2)}) async-start(bf16[32,256,32]{1,2,0:T(8,128)(2,1)} %broadcast_in_dim.30), calls=%async_computation.1 | async-start | bytes 1048576 | tf_op jit(solution)/shard_map/all_to_all | solution.py:9
  231.8 16.9 %all-to-all-start = ((bf16[32,8,1024]{2,0,1:T(8,128)(2,1)}), bf16[32,8,1024]{2,0,1:T(8,128)(2,1)S(1)}, u32[]{:S(2)}, u32[]{:S(2)}) async-start(bf16[32,8,1024]{2,0,1:T(8,128)(2,1)} %copy.34), calls=%async_computation | async-start | bytes 1048576 | tf_op jit(solution)/shard_map/all_to_all | solution.py:44
  249.4 9.5 %all-to-all-start.2 = ((bf16[8,256,32]{1,2,0:T(8,128)(2,1)}), bf16[8,256,32]{1,2,0:T(8,128)(2,1)S(1)}, u32[]{:S(2)}, u32[]{:S(2)}) async-start(bf16[8,256,32]{1,2,0:T(8,128)(2,1)} %broadcast_in_dim.31), calls=%async_computation.2 | async-start | bytes 262144 | tf_op jit(solution)/shard_map/all_to_all | solution.py:9
Sparse Core Ops, SparseCore 0:
  11.2 142.7 all-gather.2
  155.8 32.8 all-gather.4
where the time goes:
time: 267 us
  waiting for transfers between devices  169 us (63%)
  local copies, waits for them, and re-layouts  32.7 us (12%)
  matrix products  28.4 us (11%)
  starting transfers between devices  17.8 us (7%)
  between operations  14.1 us (5%)
  other arithmetic  4.35 us (2%)
    all_gather x1, waiting for transfers between devices, per_device(): whole = lax.all_gather(grad_pre, 'node', axis=1, tiled=True)  141 us
    dot_general x1, matrix products, per_device(): jnp.einsum('frkc,rkic->fri', picked, tiles, preferred_element_type=jnp.fl...  24.5 us
    all_to_all x2, waiting for transfers between devices, sent_to_all(): lax.all_to_all(jnp.broadcast_to(shard[None], (size, *shard.shape)), axis,...  17.8 us
    reshape x1, local copies, waits for them, and re-layouts, per_device(): blocks = whole.reshape(feat_rows, whole.shape[1] // block_size, block_size)  14.6 us
    gather x1, local copies, waits for them, and re-layouts, per_device(): picked = jnp.take(blocks, indices, axis=1)  12.9 us
    all_to_all x2, starting transfers between devices, sent_to_all(): lax.all_to_all(jnp.broadcast_to(shard[None], (size, *shard.shape)), axis,...  10.1 us
    all_to_all x1, waiting for transfers between devices, per_device(): lax.all_to_all(aggregated, 'feat', split_axis=1, concat_axis=0, tiled=True)  9.26 us
    all_to_all x1, starting transfers between devices, per_device(): lax.all_to_all(aggregated, 'feat', split_axis=1, concat_axis=0, tiled=True)  7.57 us
  transfers between devices with their start and end apart: 5, of which 4 were waited for; matrix products, arithmetic and copies ran while one was open for 22% of the time, Pallas kernels for 0%

commit v1 on v0

--- a/solution.py
+++ b/solution.py
@@ -2,6 +2,13 @@
 import jax.numpy as jnp
 from jax import lax
 from jax.sharding import PartitionSpec as P
+
+
+def gather_over(block, axis, dim):
+    count = lax.axis_size(axis)
+    shards = jnp.stack([block for _ in range(count)])
+    shards = lax.all_to_all(shards, axis, split_axis=0, concat_axis=0)
+    return jnp.concatenate(shards, axis=dim)
 
 
 def sent_to_all(shard, axis):
@@ -28,7 +35,7 @@
 
 def per_device(out_grad, pre_act, in_act, weight, tiles, indices, counts):
     grad_pre = jnp.where(pre_act > 0, out_grad, jnp.zeros_like(out_grad))
-    whole = lax.all_gather(grad_pre, "node", axis=1, tiled=True)
+    whole = gather_over(grad_pre, "node", 1)
     feat_rows = whole.shape[0]
     block_size = tiles.shape[2]
     slot_count = tiles.shape[1]

time: 267 us -> 594 us (2.22)
  waiting for transfers between devices: 169 us -> 397 us
  local copies, waits for them, and re-layouts: 32.7 us -> 86.5 us
  starting transfers between devices: 17.8 us -> 64.9 us
    all_to_all x0 -> x1, waiting for transfers between devices: none -> 369 us  [gather_over(): shards = lax.all_to_all(shards, axis, split_axis=0, concat_axis=0)]
    all_gather x1 -> x0, waiting for transfers between devices: 141 us -> none  [per_device(): whole = lax.all_gather(grad_pre, 'node', axis=1, tiled=True)]
    another operation x0 -> x3, local copies, waits for them, and re-layouts: none -> 50.1 us  [the longest x2 44.1 us: per_device(): blocks = whole.reshape(feat_rows, whole.shape[1] // block_size, block_size)]
    all_to_all x2, starting transfers between devices: 10.1 us -> 44.9 us  [sent_to_all(): lax.all_to_all(jnp.broadcast_to(shard[None], (size, *shard.shape)), axis,...]
    all_to_all x0 -> x1, starting transfers between devices: none -> 12.1 us  [gather_over(): shards = lax.all_to_all(shards, axis, split_axis=0, concat_axis=0)]
  transfers between devices with their start and end apart: 5 -> 5, of which waited for: 4 -> 4; matrix products, arithmetic and copies ran while one was open for 22% -> 17% of each run, Pallas kernels for 0% -> 0%
where the time goes in v1:
time: 594 us; the launch traced here: 592 us
  waiting for transfers between devices  397 us (67%)
  local copies, waits for them, and re-layouts  86.5 us (15%)
  starting transfers between devices  64.9 us (11%)
  matrix products  28.2 us (5%)
  between operations  14.2 us (2%)
    all_to_all x1, waiting for transfers between devices, gather_over(): shards = lax.all_to_all(shards, axis, split_axis=0, concat_axis=0)  369 us
    all_to_all x2, starting transfers between devices, sent_to_all(): lax.all_to_all(jnp.broadcast_to(shard[None], (size, *shard.shape)), axis,...  44.9 us
    another operation x2, local copies, waits for them, and re-layouts, per_device(): blocks = whole.reshape(feat_rows, whole.shape[1] // block_size, block_size)  44.1 us
    dot_general x1, matrix products, per_device(): jnp.einsum('frkc,rkic->fri', picked, tiles, preferred_element_type=jnp.fl...  24.3 us
    reshape x1, local copies, waits for them, and re-layouts, gather_over(): return jnp.concatenate(shards, axis=dim)  18.5 us
    all_to_all x2, waiting for transfers between devices, sent_to_all(): lax.all_to_all(jnp.broadcast_to(shard[None], (size, *shard.shape)), axis,...  17.8 us
    gather x1, local copies, waits for them, and re-layouts, per_device(): picked = jnp.take(blocks, indices, axis=1)  12.7 us
    all_to_all x1, starting transfers between devices, gather_over(): shards = lax.all_to_all(shards, axis, split_axis=0, concat_axis=0)  12.1 us
  transfers between devices with their start and end apart: 5, of which 4 were waited for; matrix products, arithmetic and copies ran while one was open for 17% of the time, Pallas kernels for 0%

profile of v1, /device:TPU:1, one launch (start us, length us, event | category | flops | bytes accessed | tf_op | source)
XLA Modules:
  0.0 592.1 jit_solution(5452175889187635882)
XLA Ops:
  7.2 1.3 compare_select_fusion
  8.5 5.9 %stack.2 = bf16[32,32,8192]{2,1,0:T(8,128)(2,1)} broadcast(bf16[32,8192]{1,0:T(8,128)(2,1)S(1)} %compare_select_fusion), dimensions={1,2} | broadcast | bytes 17301504 | tf_op jit(solution)/shard_map/stack | solution.py:9
  14.4 12.1 %all-to-all-start = ((bf16[32,32,8192]{2,1,0:T(8,128)(2,1)}), bf16[32,32,8192]{2,1,0:T(8,128)(2,1)}, u32[]{:S(2)}, u32[]{:S(2)}) async-start(bf16[32,32,8192]{2,1,0:T(8,128)(2,1)} %stack.2), calls=%async_computation | async-start | bytes 33554432 | tf_op jit(solution)/shard_map/all_to_all | solution.py:10
  26.6 0.7 all-gather.2.cloned.1.call-update
  27.7 369.1 %all-to-all-done = bf16[32,32,8192]{2,1,0:T(8,128)(2,1)} async-done(((bf16[32,32,8192]{2,1,0:T(8,128)(2,1)}), bf16[32,32,8192]{2,1,0:T(8,128)(2,1)}, u32[]{:S(2)}, u32[]{:S(2)}) %all-to-all-start) | async-done | bytes 16777248 | tf_op jit(solution)/shard_map/all_to_all | solution.py:10
  396.8 18.5 %copy.22 = bf16[32,32,8192]{2,1,0:T(8,128)(2,1)} copy(bf16[32,32,8192]{2,0,1:T(8,128)(2,1)} %bitcast) | data formatting | bytes 33554432 | tf_op jit(solution)/shard_map/reshape | solution.py:11
  415.4 25.6 %reshape_reshape.3 = bf16[32,2048,128]{2,1,0:T(8,128)(2,1)} reshape(bf16[32,32,8192]{2,1,0:T(8,128)(2,1)} %copy.22) | data formatting | bytes 33554432 | tf_op jit(solution)/shard_map/reshape;reshape | solution.py:43
  441.0 18.5 %copy.24 = bf16[32,2048,128]{2,0,1:T(8,128)(2,1)} copy(bf16[32,2048,128]{2,1,0:T(8,128)(2,1)} %reshape_reshape.3) | data formatting | bytes 33554432 | tf_op jit(solution)/shard_map/reshape;reshape | solution.py:43
  459.5 12.7 %gather_fusion = bf16[1536,32,128]{2,1,0:T(8,128)(2,1)} fusion(bf16[32,2048,128]{2,0,1:T(8,128)(2,1)} %copy.24, s32[2048]{0:T(1024)S(1)} %pad_clamp_fusion), kind=kCustom, calls=%fused_computation | custom fusion | bytes 25171968 | tf_op jit(solution)/shard_map/jit(_take)/gather | solution.py:44
  472.2 24.3 %fusion.10 = bf16[64,32,128]{2,1,0:T(8,128)(2,1)S(1)} fusion(bf16[64,24,128,128]{3,2,1,0:T(8,128)(2,1)} %param.11, bf16[64,24,32,128]{3,2,1,0:T(8,128)(2,1)} %bitcast.36, pred[64,24]{1,0:T(8,128)(4,1)S(1)} %copy.21, bf16[64,24]{1,0:T(8,128)(2,1)S(1)} %fusion.18), kind=kOutput, calls=%fused_computation.10 | convolution fusion | flops 1623457792 | bytes 63443456 | tf_op jit(solution)/shard_map/frkc,rkic->fri/dot_general | solution.py:48
  496.5 3.5 fusion.15
  500.1 0.8 broadcast_in_dim.30
  500.9 40.7 %all-to-all-start.2 = ((bf16[32,256,32]{1,2,0:T(8,128)(2,1)}), bf16[32,256,32]{1,2,0:T(8,128)(2,1)S(1)}, u32[]{:S(2)}, u32[]{:S(2)}) async-start(bf16[32,256,32]{1,2,0:T(8,128)(2,1)} %broadcast_in_dim.30), calls=%async_computation.2 | async-start | bytes 1048576 | tf_op jit(solution)/shard_map/all_to_all | solution.py:16
  541.8 0.2 convert_element_type.47
  542.1 1.1 copy.26
  543.1 13.9 %all-to-all-done.2 = bf16[32,256,32]{1,2,0:T(8,128)(2,1)S(1)} async-done(((bf16[32,256,32]{1,2,0:T(8,128)(2,1)}), bf16[32,256,32]{1,2,0:T(8,128)(2,1)S(1)}, u32[]{:S(2)}, u32[]{:S(2)}) %all-to-all-start.2) | async-done | bytes 524320 | tf_op jit(solution)/shard_map/all_to_all | solution.py:16
  557.1 7.8 %all-to-all-start.1 = ((bf16[32,8,1024]{2,0,1:T(8,128)(2,1)}), bf16[32,8,1024]{2,0,1:T(8,128)(2,1)S(1)}, u32[]{:S(2)}, u32[]{:S(2)}) async-start(bf16[32,8,1024]{2,0,1:T(8,128)(2,1)} %copy.26), calls=%async_computation.1 | async-start | bytes 1048576 | tf_op jit(solution)/shard_map/all_to_all | solution.py:51
  565.0 9.3 %all-to-all-done.1 = bf16[32,8,1024]{2,0,1:T(8,128)(2,1)S(1)} async-done(((bf16[32,8,1024]{2,0,1:T(8,128)(2,1)}), bf16[32,8,1024]{2,0,1:T(8,128)(2,1)S(1)}, u32[]{:S(2)}, u32[]{:S(2)}) %all-to-all-start.1) | async-done | bytes 524320 | tf_op jit(solution)/shard_map/all_to_all | solution.py:51
  574.2 0.7 broadcast_in_dim.31
  574.9 4.2 all-to-all-start.3
  579.1 0.4 fusion.13
  579.5 1.0 copy.28
  580.5 3.9 all-to-all-done.3
  584.4 0.8 copy.29
  (18 shorter events, 0.8 us)
Async XLA Ops:
  7.2 572.0 %copy-start = (bf16[256,256]{1,0:T(8,128)(2,1)S(1)}, bf16[256,256]{1,0:T(8,128)(2,1)}, u32[]{:S(2)}) copy-start(bf16[256,256]{1,0:T(8,128)(2,1)} %param.10) | copy-start | bytes 393220
  14.4 12.9 %copy-start.1 = (s32[64,24]{0,1:T(8,128)S(1)}, s32[64,24]{0,1:T(8,128)}, u32[]{:S(2)}) copy-start(s32[64,24]{0,1:T(8,128)} %param.12) | copy-start | bytes 18436
  14.4 13.2 %copy-start.2 = (s32[64]{0:T(128)S(1)}, s32[64]{0:T(128)}, u32[]{:S(2)}) copy-start(s32[64]{0:T(128)} %param.13) | copy-start | bytes 772
  14.4 382.4 %all-to-all-start = ((bf16[32,32,8192]{2,1,0:T(8,128)(2,1)}), bf16[32,32,8192]{2,1,0:T(8,128)(2,1)}, u32[]{:S(2)}, u32[]{:S(2)}) async-start(bf16[32,32,8192]{2,1,0:T(8,128)(2,1)} %stack.2), calls=%async_computation | async-start | bytes 33554432 | tf_op jit(solution)/shard_map/all_to_all | solution.py:10
  26.6 470.0 %all-gather.2.cloned.1.call-start = ((), (), s32[]{:S(2)}) async-start(), calls=%async_computation.4 | async-start | bytes 4718592 | tf_op jit(solution)/shard_map/all_gather | solution.py:53
  500.9 56.1 %all-to-all-start.2 = ((bf16[32,256,32]{1,2,0:T(8,128)(2,1)}), bf16[32,256,32]{1,2,0:T(8,128)(2,1)S(1)}, u32[]{:S(2)}, u32[]{:S(2)}) async-start(bf16[32,256,32]{1,2,0:T(8,128)(2,1)} %broadcast_in_dim.30), calls=%async_computation.2 | async-start | bytes 1048576 | tf_op jit(solution)/shard_map/all_to_all | solution.py:16
  557.1 17.2 %all-to-all-start.1 = ((bf16[32,8,1024]{2,0,1:T(8,128)(2,1)}), bf16[32,8,1024]{2,0,1:T(8,128)(2,1)S(1)}, u32[]{:S(2)}, u32[]{:S(2)}) async-start(bf16[32,8,1024]{2,0,1:T(8,128)(2,1)} %copy.26), calls=%async_computation.1 | async-start | bytes 1048576 | tf_op jit(solution)/shard_map/all_to_all | solution.py:51
  574.9 9.5 %all-to-all-start.3 = ((bf16[8,256,32]{1,2,0:T(8,128)(2,1)}), bf16[8,256,32]{1,2,0:T(8,128)(2,1)S(1)}, u32[]{:S(2)}, u32[]{:S(2)}) async-start(bf16[8,256,32]{1,2,0:T(8,128)(2,1)} %broadcast_in_dim.31), calls=%async_computation.3 | async-start | bytes 262144 | tf_op jit(solution)/shard_map/all_to_all | solution.py:16
Sparse Core Ops, SparseCore 0:
  29.2 36.6 all-gather.1
